TPU v7x, 256 devices: a whole 4x4x8 slice. The times are simulated.
256 devices in a mesh: tm: 64 (over y, z, core), col: 4 (over x).
Axes of the slice: x: 4, y: 4, z: 8, core: 2. Of those that a mesh axis runs over, the one named last changes fastest.
Arguments:
- transition: bfloat16 [512, 256, 256], P('tm', 'col'), may hold values from -1 to 1, as said below
- drive: float32 [512, 16, 256], P('tm', 'col'), may hold values from -0.3125 to 0.3125
- smoother_gain: bfloat16 [512, 256, 256], P('tm', 'col'), may hold values from -1 to 1, as said below
- dynamics: float32 [256, 256], replicated, may hold values from -0.375 to 0.375
- initial_mean: float32 [16, 256], P('col'), may hold values from -6 to 6
Outputs:
- filtered_mean: float32 [512, 16, 256], P('tm', 'col')
- smoothed_mean: float32 [512, 16, 256], P('tm', 'col')
Inputs may be any that keep to these rules, and one draw needn't show every extreme that they name: `transition`: every step operator is a per-channel diagonal plus a dense full-rank part. `smoother_gain`: every gain is a per-channel diagonal plus a dense full-rank part.
All inputs are finite; a program needn't handle non-finite values.
Results may differ from a plain program's by a relative error of at most 0.0018.
Values may be sent and summed in bfloat16 or wider, within the bound.
No kernel may reach another device: no remote copies, remote signals or barrier semaphores. Data moves between devices by JAX's collectives and lax.ppermute only.
A program may use at most 128 MiB of HBM per device.

v0:
```python
import jax
import jax.numpy as jnp
from jax import lax
from jax.sharding import PartitionSpec as P

highest = lax.Precision.HIGHEST


def prefix(part, axis, combine, identity, reverse):
    count = lax.axis_size(axis)
    place = lax.axis_index(axis)
    ahead = count - 1 - place if reverse else place
    gathered = jax.tree.map(lambda a: lax.all_gather(a, axis), part)
    state = jax.tree.map(lambda a, e: jnp.zeros_like(a) + jnp.asarray(e, a.dtype), part, identity)

    def one(lap, state):
        source = count - 1 - lap if reverse else lap
        return combine(
            state, jax.tree.map(lambda a: lax.dynamic_index_in_dim(a, source, 0, False), gathered)
        )

    return lax.fori_loop(0, ahead, one, state)


def widen(matrix):
    return matrix.astype(jnp.float32)


def product(left, right):
    return jnp.dot(left, right, precision=highest, preferred_element_type=jnp.float32)


def combine_pair(earlier, later):
    first_op, first_vec = earlier
    second_op, second_vec = later
    return (product(first_op, second_op), product(first_vec, second_op) + second_vec)


def right_product(whole, seed, upward):
    count = whole.shape[0]

    def turn(step, current):
        position = step + 1 if upward else count - 2 - step
        return product(current, widen(whole[position]))

    return lax.fori_loop(0, count - 1, turn, widen(seed))


def run_forward(begin, operators, pushes, keep_all):

    def forward_step(state, inputs):
        operator, push = inputs
        state = product(state, widen(operator)) + push
        return (state, state if keep_all else None)

    return lax.scan(forward_step, begin, (operators, pushes))


def run_backward(begin, gains, corrections, keep_all):

    def backward_step(state, inputs):
        gain_now, corr_now = inputs
        state = product(state, widen(gain_now)) + corr_now
        return (state, state if keep_all else None)

    return lax.scan(backward_step, begin, (gains, corrections), reverse=True)


def corrections_of(filtered, gains, dynamics):

    def correct_step(carry, inputs):
        mean_now, gain_now = inputs
        projected = product(mean_now, dynamics)
        return (carry, mean_now - product(projected, widen(gain_now)))

    _, correction = lax.scan(correct_step, jnp.float32(0.0), (filtered, gains))
    return correction


def local(transition, drive, smoother_gain, dynamics, initial_mean):
    steps_dev = transition.shape[0]
    height = transition.shape[1]
    whole_trans, whole_gains = (
        lax.all_gather(transition, "col", axis=1, tiled=True),
        lax.all_gather(smoother_gain, "col", axis=1, tiled=True),
    )
    last_device = lax.axis_index("tm") == lax.axis_size("tm") - 1
    positions = jnp.arange(steps_dev)
    keep = jnp.logical_not(jnp.logical_and(last_device, positions == steps_dev - 1))
    whole_gains = jnp.where(keep[:, None, None], whole_gains, jnp.zeros_like(whole_gains))
    start = lax.axis_index("col") * height
    seed_trans = lax.dynamic_slice_in_dim(whole_trans[0], start, height, 0)
    seed_gains = lax.dynamic_slice_in_dim(whole_gains[steps_dev - 1], start, height, 0)
    part_trans = right_product(whole_trans, seed_trans, True)
    part_gains = right_product(whole_gains, seed_gains, False)
    block_trans, block_gains = (
        lax.all_gather(part_trans, "col", axis=0, tiled=True),
        lax.all_gather(part_gains, "col", axis=0, tiled=True),
    )
    empty = jnp.zeros_like(initial_mean)
    block_drive, _ = run_forward(empty, whole_trans, drive, False)
    ident = jnp.eye(block_trans.shape[0], dtype=jnp.float32)
    prefix_op, prefix_vec = prefix(
        (block_trans, block_drive), "tm", combine_pair, (ident, empty), False
    )
    incoming = product(initial_mean, prefix_op) + prefix_vec
    _, filtered = run_forward(incoming, whole_trans, drive, True)
    correction = corrections_of(filtered, whole_gains, dynamics)
    block_corr, _ = run_backward(empty, whole_gains, correction, False)
    _, next_state = prefix((block_gains, block_corr), "tm", combine_pair, (ident, empty), True)
    _, smoothed = run_backward(next_state, whole_gains, correction, True)
    return (filtered, smoothed)


def solution(mesh):
    placed = (P("tm", "col", None), P("tm", "col", None), P("tm", "col", None), P(), P("col", None))
    return jax.shard_map(
        local,
        mesh=mesh,
        in_specs=placed,
        out_specs=(P("tm", "col", None), P("tm", "col", None)),
        check_vma=False,
    )
```

profile of v0, /device:TPU:1, one launch (start us, length us, event | category | flops | bytes accessed | tf_op | source)
XLA Modules:
  0.0 507.6 jit_solution(2195301427567029358)
XLA Ops:
  8.7 29.4 %all-gather.13.cloned.1.call-done = bf16[8,256,256]{2,1,0:T(8,128)(2,1)} async-done(((bf16[8,64,256]{2,1,0:T(8,128)(2,1)}), bf16[8,256,256]{2,1,0:T(8,128)(2,1)}) %all-gather.13.cloned.1.call-update) | async-done | bytes 1048592 | tf_op jit(solution)/shard_map/all_gather | solution.py:85
  38.2 1.4 broadcast_select_fusion
  39.6 27.5 %all-gather.11.cloned.1.call-done = bf16[8,256,256]{2,1,0:T(8,128)(2,1)} async-done(((bf16[8,64,256]{2,1,0:T(8,128)(2,1)}), bf16[8,256,256]{2,1,0:T(8,128)(2,1)}) %all-gather.11.cloned.1.call-update) | async-done | bytes 1048592 | tf_op jit(solution)/shard_map/all_gather | solution.py:84
  68.0 8.1 %while.120 = (s32[]{:T(128)}, f32[64,256]{1,0:T(8,128)S(1)}, bf16[8,256,256]{2,1,0:T(8,128)(2,1)}, s32[]{:T(128)}, s32[]{:T(128)}, /*index=5*/s32[]{:T(128)}) while((s32[]{:T(128)}, f32[64,256]{1,0:T(8,128)S(1)}, bf16[8,256,256]{2,1,0:T(8,128)(2,1)}, s32[]{:T(128)}, s32[]{:T(128)}, /*index=5*/s32[]{:T(128)}) %tuple.220), condition=%wide.region_1.2_spmd, body=%wide.region_0.1_spmd.sunk | while | flops 50331652 | bytes 393331 | solution.py:46
  76.1 10.1 %all_gather.37 = f32[256,256]{1,0:T(8,128)} all-gather(f32[64,256]{1,0:T(8,128)S(1)} %get-tuple-element.559), channel_id=1, replica_groups=mesh['tm'=64,'col'=4] {'col'}, dimensions={0}, use_global_device_ids=true | all-gather | bytes 327680 | tf_op jit(solution)/shard_map/all_gather | solution.py:97
  86.3 1.8 while.123
  88.1 10.1 %all_gather.43 = f32[256,256]{1,0:T(8,128)} all-gather(f32[64,256]{1,0:T(8,128)S(1)} %get-tuple-element.564), channel_id=1, replica_groups=mesh['tm'=64,'col'=4] {'col'}, dimensions={0}, use_global_device_ids=true | all-gather | bytes 327680 | tf_op jit(solution)/shard_map/all_gather | solution.py:98
  98.3 8.8 %while.127 = (s32[]{:T(128)}, f32[4,256]{1,0:T(4,128)S(1)}, bf16[8,256,256]{2,1,0:T(8,128)(2,1)}, f32[8,4,256]{2,1,0:T(4,128)}, s32[]{:T(128)}, /*index=5*/s32[]{:T(128)}) while((s32[]{:T(128)}, f32[4,256]{1,0:T(4,128)S(1)}, bf16[8,256,256]{2,1,0:T(8,128)(2,1)}, f32[8,4,256]{2,1,0:T(4,128)}, s32[]{:T(128)}, ...), condition=%wide.region_3.4_spmd.clone, body=%wide.region_2.3_spmd.clone.sunk | while | flops 3147779 | bytes 152655 | solution.py:56
  107.1 54.0 %all-gather.4 = f32[64,4,256]{2,1,0:T(4,128)S(1)} all-gather(f32[1,4,256]{2,1,0:T(4,128)S(1)} %bitcast.184), channel_id=3, replica_groups=mesh['tm'=64,'col'=4] {'tm'}, dimensions={0}, use_global_device_ids=true | all-gather | bytes 266240 | tf_op jit(solution)/shard_map/all_gather | solution.py:13
  161.0 30.0 %all-gather.15.cloned.1.call-done = f32[16384,256]{1,0:T(8,128)} async-done(((f32[256,256]{1,0:T(8,128)}), f32[16384,256]{1,0:T(8,128)}) %all-gather.15.cloned.1.call-update) | async-done | bytes 16777232 | tf_op jit(solution)/shard_map/all_gather | solution.py:13
  191.0 2.8 while.121
  192.2 1.6 convolution_bitcast_fusion.14
  194.2 8.8 %while.122 = (s32[]{:T(128)}, f32[4,256]{1,0:T(4,128)S(1)}, f32[8,4,256]{2,1,0:T(4,128)S(1)}, bf16[8,256,256]{2,1,0:T(8,128)(2,1)}, f32[8,4,256]{2,1,0:T(4,128)}, /*index=5*/s32[]{:T(128)}) while((s32[]{:T(128)}, f32[4,256]{1,0:T(4,128)S(1)}, f32[8,4,256]{2,1,0:T(4,128)S(1)}, bf16[8,256,256]{2,1,0:T(8,128)(2,1)}, f32[8,4,256]{2,1,0:T(4,128)}, ...), condition=%wide.region_7.8_spmd, body=%wide.region_6.7_spmd.sunk | while | flops 3146754 | bytes 156741 | solution.py:56
  203.0 3.4 while.124
  206.4 1.6 while.128
  208.0 216.1 %all-gather.5 = f32[64,4,256]{2,1,0:T(4,128)S(1)} all-gather(f32[1,4,256]{2,1,0:T(4,128)S(1)} %bitcast.183), channel_id=5, replica_groups=mesh['tm'=64,'col'=4] {'tm'}, dimensions={0}, use_global_device_ids=true | all-gather | bytes 266240 | tf_op jit(solution)/shard_map/all_gather | solution.py:13
  424.0 74.7 %while.125 = (s32[]{:T(128)}, f32[4,256]{1,0:T(4,128)S(1)}, s32[]{:T(128)}, f32[64,256,256]{2,1,0:T(8,128)}, f32[64,4,256]{2,1,0:T(4,128)S(1)}, /*index=5*/s32[]{:T(128)}, s32[]{:T(128)}, s32[]{:T(128)}, s32[]{:T(128)}) while((s32[]{:T(128)}, f32[4,256]{1,0:T(4,128)S(1)}, s32[]{:T(128)}, f32[64,256,256]{2,1,0:T(8,128)}, ...), condition=%wide.region_15.16_spmd, body=%wide.region_14.15_spmd.sunk | while | flops 3146758 | bytes 283787 | solution.py:22
  425.3 1.2 fusion.107
  427.7 1.2 fusion.107
  428.9 1.2 fusion.107
  430.1 1.2 fusion.107
  431.3 1.2 fusion.107
  432.5 1.2 fusion.107
  433.7 1.2 fusion.107
  434.9 1.2 fusion.107
  436.1 1.2 fusion.107
  437.3 1.2 fusion.107
  438.5 1.2 fusion.107
  439.7 1.2 fusion.107
  440.9 1.2 fusion.107
  442.1 1.2 fusion.107
  443.3 1.2 fusion.107
  444.5 1.2 fusion.107
  445.7 1.2 fusion.107
  446.9 1.2 fusion.107
  448.2 1.2 fusion.107
  450.6 1.2 fusion.107
  451.8 1.2 fusion.107
  453.0 1.2 fusion.107
  454.2 1.2 fusion.107
  455.4 1.2 fusion.107
  456.6 1.2 fusion.107
  457.8 1.2 fusion.107
  459.0 1.2 fusion.107
  460.2 1.2 fusion.107
  461.4 1.2 fusion.107
  462.6 1.2 fusion.107
  463.8 1.2 fusion.107
  465.0 1.2 fusion.107
  466.2 1.2 fusion.107
  467.4 1.2 fusion.107
  468.6 1.2 fusion.107
  469.8 1.2 fusion.107
  471.1 1.2 fusion.107
  473.5 1.2 fusion.107
  474.7 1.2 fusion.107
  475.9 1.2 fusion.107
  477.1 1.2 fusion.107
  478.3 1.2 fusion.107
  479.5 1.2 fusion.107
  480.7 1.2 fusion.107
  481.9 1.2 fusion.107
  483.1 1.2 fusion.107
  498.8 1.6 while.126
  (219 shorter events, 57.3 us)
Async XLA Ops:
  7.2 186.6 %copy-start = (f32[4,256]{1,0:T(4,128)S(1)}, f32[4,256]{1,0:T(4,128)}, u32[]{:S(2)}) copy-start(f32[4,256]{1,0:T(4,128)} %param.27) | copy-start | bytes 12292
  7.2 195.8 %copy-start.1 = (f32[256,256]{1,0:T(8,128)S(1)}, f32[256,256]{1,0:T(8,128)}, u32[]{:S(2)}) copy-start(f32[256,256]{1,0:T(8,128)} %param.26) | copy-start | bytes 786436
  7.2 31.0 %all-gather.13.cloned.1.call-start = ((), (), s32[]{:S(2)}) async-start(), calls=%async_computation.1 | async-start | bytes 1310720 | tf_op jit(solution)/shard_map/all_gather | solution.py:85
  7.9 59.1 %all-gather.11.cloned.1.call-start = ((), (), s32[]{:S(2)}) async-start(), calls=%async_computation | async-start | bytes 1310720 | tf_op jit(solution)/shard_map/all_gather | solution.py:84
  8.7 182.3 %all-gather.15.cloned.1.call-start = ((), (), s32[]{:S(2)}) async-start(), calls=%async_computation.2 | async-start | bytes 17039360 | tf_op jit(solution)/shard_map/all_gather | solution.py:13
  86.2 337.8 %all-gather.17.cloned.1.call-start = ((), (), s32[]{:S(2)}) async-start(), calls=%async_computation.3 | async-start | bytes 17039360 | tf_op jit(solution)/shard_map/all_gather | solution.py:13
  206.4 294.0 %copy-start.2 = (f32[8,4,256]{2,1,0:T(4,128)}, f32[8,4,256]{2,1,0:T(4,128)S(1)}, u32[]{:S(2)}) copy-start(f32[8,4,256]{2,1,0:T(4,128)S(1)} %get-tuple-element.1153) | copy-start | bytes 98308
  500.4 0.7 copy-start.3
Sparse Core Ops, SparseCore 0:
  9.8 28.3 all-gather.12
  40.0 27.0 all-gather.10
  86.4 104.5 all-gather.14
  193.6 96.3 all-gather.16
where the time goes:
time: 512 us; the launch traced here: 508 us
  blocking collectives  290 us (57%)
  matrix products  109 us (21%)
  waiting for transfers between devices  88.3 us (17%)
  between operations  13.9 us (3%)
    all_gather x2, blocking collectives, prefix(): gathered = jax.tree.map(lambda a: lax.all_gather(a, axis), part)  270 us
    dot_general x127, matrix products, product(): jnp.dot(left, right, precision=highest, preferred_element_type=jnp.float32)  109 us
    all_gather x2, waiting for transfers between devices, prefix(): gathered = jax.tree.map(lambda a: lax.all_gather(a, axis), part)  30 us
    all_gather x1, waiting for transfers between devices, local(): lax.all_gather(smoother_gain, 'col', axis=1, tiled=True)  29.4 us
    all_gather x1, waiting for transfers between devices, local(): lax.all_gather(transition, 'col', axis=1, tiled=True)  27.5 us
  transfers between devices with their start and end apart: 4, of which 3 were waited for; matrix products, arithmetic and copies ran while one was open for 6% of the time, Pallas kernels for 0%

commit v1 on v0

--- a/solution.py
+++ b/solution.py
@@ -4,6 +4,13 @@
 from jax.sharding import PartitionSpec as P
 
 highest = lax.Precision.HIGHEST
+
+
+def start_sample(t0, axis_k):
+    prior = jnp.stack([t0 for _ in range(lax.psum(1, "col"))])
+    current_arr = lax.all_to_all(prior, "col", 0, 0)
+    moved = jnp.concatenate(current_arr, axis_k)
+    return moved
 
 
 def prefix(part, axis, combine, identity, reverse):
@@ -82,7 +89,7 @@
     height = transition.shape[1]
     whole_trans, whole_gains = (
         lax.all_gather(transition, "col", axis=1, tiled=True),
-        lax.all_gather(smoother_gain, "col", axis=1, tiled=True),
+        start_sample(smoother_gain, axis_k=1),
     )
     last_device = lax.axis_index("tm") == lax.axis_size("tm") - 1
     positions = jnp.arange(steps_dev)

time: 512 us -> 485 us (0.947)
  waiting for transfers between devices: 88.3 us -> 55.6 us
    all_gather x1 -> x0, waiting for transfers between devices: 29.4 us -> none  [local(): lax.all_gather(smoother_gain, 'col', axis=1, tiled=True)]
    all_gather x1, waiting for transfers between devices: 27.5 us -> 11.3 us  [local(): lax.all_gather(transition, 'col', axis=1, tiled=True)]
    all_to_all x0 -> x1, waiting for transfers between devices: none -> 13.3 us  [start_sample(): current_arr = lax.all_to_all(prior, 'col', 0, 0)]
where the time goes in v1:
time: 485 us; the launch traced here: 480 us
  blocking collectives  290 us (60%)
  matrix products  109 us (22%)
  waiting for transfers between devices  55.6 us (11%)
  between operations  13.9 us (3%)
  starting transfers between devices  4.91 us (1%)
    all_gather x2, blocking collectives, prefix(): gathered = jax.tree.map(lambda a: lax.all_gather(a, axis), part)  269 us
    dot_general x127, matrix products, product(): jnp.dot(left, right, precision=highest, preferred_element_type=jnp.float32)  109 us
    all_gather x2, waiting for transfers between devices, prefix(): gathered = jax.tree.map(lambda a: lax.all_gather(a, axis), part)  30.2 us
    all_to_all x1, waiting for transfers between devices, start_sample(): current_arr = lax.all_to_all(prior, 'col', 0, 0)  13.3 us
    all_gather x1, waiting for transfers between devices, local(): lax.all_gather(transition, 'col', axis=1, tiled=True)  11.3 us
    all_gather x1, blocking collectives, local(): lax.all_gather(part_trans, 'col', axis=0, tiled=True)  10.5 us
    all_gather x1, blocking collectives, local(): lax.all_gather(part_gains, 'col', axis=0, tiled=True)  10.1 us
  transfers between devices with their start and end apart: 4, of which 3 were waited for; matrix products, arithmetic and copies ran while one was open for 6% of the time, Pallas kernels for 0%

profile of v1, /device:TPU:1, one launch (start us, length us, event | category | flops | bytes accessed | tf_op | source)
XLA Modules:
  0.0 480.2 jit_solution(9722567483839983133)
XLA Ops:
  7.9 2.1 stack.2
  10.0 4.8 %all-to-all-start = ((bf16[4,8,64,256]{3,2,1,0:T(8,128)(2,1)}), bf16[4,8,64,256]{3,2,1,0:T(8,128)(2,1)S(1)}, u32[]{:S(2)}, u32[]{:S(2)}) async-start(bf16[4,8,64,256]{3,2,1,0:T(8,128)(2,1)} %stack.2), calls=%async_computation | async-start | bytes 2097152 | tf_op jit(solution)/shard_map/all_to_all | solution.py:11
  14.9 13.3 %all-to-all-done = bf16[4,8,64,256]{3,2,1,0:T(8,128)(2,1)S(1)} async-done(((bf16[4,8,64,256]{3,2,1,0:T(8,128)(2,1)}), bf16[4,8,64,256]{3,2,1,0:T(8,128)(2,1)S(1)}, u32[]{:S(2)}, u32[]{:S(2)}) %all-to-all-start) | async-done | bytes 1048608 | tf_op jit(solution)/shard_map/all_to_all | solution.py:11
  28.4 11.3 %all-gather.10.cloned.1.call-done = bf16[8,256,256]{2,1,0:T(8,128)(2,1)} async-done(((bf16[8,64,256]{2,1,0:T(8,128)(2,1)}), bf16[8,256,256]{2,1,0:T(8,128)(2,1)}) %all-gather.10.cloned.1.call-update) | async-done | bytes 1048592 | tf_op jit(solution)/shard_map/all_gather | solution.py:91
  40.7 8.1 %while.120 = (s32[]{:T(128)}, f32[64,256]{1,0:T(8,128)S(1)}, bf16[8,256,256]{2,1,0:T(8,128)(2,1)}, s32[]{:T(128)}, s32[]{:T(128)}, /*index=5*/s32[]{:T(128)}) while((s32[]{:T(128)}, f32[64,256]{1,0:T(8,128)S(1)}, bf16[8,256,256]{2,1,0:T(8,128)(2,1)}, s32[]{:T(128)}, s32[]{:T(128)}, /*index=5*/s32[]{:T(128)}) %tuple.220), condition=%wide.region_1.2_spmd, body=%wide.region_0.1_spmd.sunk | while | flops 50331652 | bytes 393331 | solution.py:53
  48.8 10.5 %all_gather.34 = f32[256,256]{1,0:T(8,128)} all-gather(f32[64,256]{1,0:T(8,128)S(1)} %get-tuple-element.559), channel_id=1, replica_groups=mesh['tm'=64,'col'=4] {'col'}, dimensions={0}, use_global_device_ids=true | all-gather | bytes 327680 | tf_op jit(solution)/shard_map/all_gather | solution.py:104
  59.4 1.8 while.123
  61.2 10.1 %all_gather.39 = f32[256,256]{1,0:T(8,128)} all-gather(f32[64,256]{1,0:T(8,128)S(1)} %get-tuple-element.564), channel_id=1, replica_groups=mesh['tm'=64,'col'=4] {'col'}, dimensions={0}, use_global_device_ids=true | all-gather | bytes 327680 | tf_op jit(solution)/shard_map/all_gather | solution.py:105
  71.4 8.8 %while.127 = (s32[]{:T(128)}, f32[4,256]{1,0:T(4,128)S(1)}, bf16[8,256,256]{2,1,0:T(8,128)(2,1)}, f32[8,4,256]{2,1,0:T(4,128)}, s32[]{:T(128)}, /*index=5*/s32[]{:T(128)}) while((s32[]{:T(128)}, f32[4,256]{1,0:T(4,128)S(1)}, bf16[8,256,256]{2,1,0:T(8,128)(2,1)}, f32[8,4,256]{2,1,0:T(4,128)}, s32[]{:T(128)}, ...), condition=%wide.region_3.4_spmd.clone, body=%wide.region_2.3_spmd.clone.sunk | while | flops 3147779 | bytes 152655 | solution.py:63
  80.2 53.2 %all-gather.4 = f32[64,4,256]{2,1,0:T(4,128)S(1)} all-gather(f32[1,4,256]{2,1,0:T(4,128)S(1)} %bitcast.188), channel_id=3, replica_groups=mesh['tm'=64,'col'=4] {'tm'}, dimensions={0}, use_global_device_ids=true | all-gather | bytes 266240 | tf_op jit(solution)/shard_map/all_gather | solution.py:20
  133.5 30.2 %all-gather.12.cloned.1.call-done = f32[16384,256]{1,0:T(8,128)} async-done(((f32[256,256]{1,0:T(8,128)}), f32[16384,256]{1,0:T(8,128)}) %all-gather.12.cloned.1.call-update) | async-done | bytes 16777232 | tf_op jit(solution)/shard_map/all_gather | solution.py:20
  163.7 2.8 while.121
  164.9 1.6 convolution_bitcast_fusion.14
  166.8 8.8 %while.122 = (s32[]{:T(128)}, f32[4,256]{1,0:T(4,128)S(1)}, f32[8,4,256]{2,1,0:T(4,128)S(1)}, bf16[8,256,256]{2,1,0:T(8,128)(2,1)}, f32[8,4,256]{2,1,0:T(4,128)}, /*index=5*/s32[]{:T(128)}) while((s32[]{:T(128)}, f32[4,256]{1,0:T(4,128)S(1)}, f32[8,4,256]{2,1,0:T(4,128)S(1)}, bf16[8,256,256]{2,1,0:T(8,128)(2,1)}, f32[8,4,256]{2,1,0:T(4,128)}, ...), condition=%wide.region_7.8_spmd, body=%wide.region_6.7_spmd.sunk | while | flops 3146754 | bytes 156741 | solution.py:63
  175.7 3.4 while.124
  179.1 1.6 while.128
  180.7 216.1 %all-gather.5 = f32[64,4,256]{2,1,0:T(4,128)S(1)} all-gather(f32[1,4,256]{2,1,0:T(4,128)S(1)} %bitcast.187), channel_id=5, replica_groups=mesh['tm'=64,'col'=4] {'tm'}, dimensions={0}, use_global_device_ids=true | all-gather | bytes 266240 | tf_op jit(solution)/shard_map/all_gather | solution.py:20
  396.7 74.7 %while.125 = (s32[]{:T(128)}, f32[4,256]{1,0:T(4,128)S(1)}, s32[]{:T(128)}, f32[64,256,256]{2,1,0:T(8,128)}, f32[64,4,256]{2,1,0:T(4,128)S(1)}, /*index=5*/s32[]{:T(128)}, s32[]{:T(128)}, s32[]{:T(128)}, s32[]{:T(128)}) while((s32[]{:T(128)}, f32[4,256]{1,0:T(4,128)S(1)}, s32[]{:T(128)}, f32[64,256,256]{2,1,0:T(8,128)}, ...), condition=%wide.region_15.16_spmd, body=%wide.region_14.15_spmd.sunk | while | flops 3146758 | bytes 283787 | solution.py:29
  397.9 1.2 fusion.107
  399.1 1.2 fusion.107
  400.3 1.2 fusion.107
  401.5 1.2 fusion.107
  402.7 1.2 fusion.107
  404.0 1.2 fusion.107
  405.2 1.2 fusion.107
  406.4 1.2 fusion.107
  407.6 1.2 fusion.107
  408.8 1.2 fusion.107
  410.0 1.2 fusion.107
  411.2 1.2 fusion.107
  412.4 1.2 fusion.107
  414.8 1.2 fusion.107
  416.0 1.2 fusion.107
  417.2 1.2 fusion.107
  418.4 1.2 fusion.107
  419.6 1.2 fusion.107
  420.8 1.2 fusion.107
  422.0 1.2 fusion.107
  423.2 1.2 fusion.107
  424.4 1.2 fusion.107
  425.6 1.2 fusion.107
  426.9 1.2 fusion.107
  428.1 1.2 fusion.107
  429.3 1.2 fusion.107
  430.5 1.2 fusion.107
  431.7 1.2 fusion.107
  432.9 1.2 fusion.107
  434.1 1.2 fusion.107
  435.3 1.2 fusion.107
  437.7 1.2 fusion.107
  438.9 1.2 fusion.107
  440.1 1.2 fusion.107
  441.3 1.2 fusion.107
  442.5 1.2 fusion.107
  443.7 1.2 fusion.107
  444.9 1.2 fusion.107
  446.1 1.2 fusion.107
  447.3 1.2 fusion.107
  448.5 1.2 fusion.107
  449.8 1.2 fusion.107
  451.0 1.2 fusion.107
  452.2 1.2 fusion.107
  453.4 1.2 fusion.107
  471.5 1.6 while.126
  (220 shorter events, 57.9 us)
Async XLA Ops:
  7.2 159.3 %copy-start = (f32[4,256]{1,0:T(4,128)S(1)}, f32[4,256]{1,0:T(4,128)}, u32[]{:S(2)}) copy-start(f32[4,256]{1,0:T(4,128)} %param.27) | copy-start | bytes 12292
  7.2 168.5 %copy-start.1 = (f32[256,256]{1,0:T(8,128)S(1)}, f32[256,256]{1,0:T(8,128)}, u32[]{:S(2)}) copy-start(f32[256,256]{1,0:T(8,128)} %param.26) | copy-start | bytes 786436
  7.2 32.6 %all-gather.10.cloned.1.call-start = ((), (), s32[]{:S(2)}) async-start(), calls=%async_computation.1 | async-start | bytes 1310720 | tf_op jit(solution)/shard_map/all_gather | solution.py:91
  10.0 18.2 %all-to-all-start = ((bf16[4,8,64,256]{3,2,1,0:T(8,128)(2,1)}), bf16[4,8,64,256]{3,2,1,0:T(8,128)(2,1)S(1)}, u32[]{:S(2)}, u32[]{:S(2)}) async-start(bf16[4,8,64,256]{3,2,1,0:T(8,128)(2,1)} %stack.2), calls=%async_computation | async-start | bytes 2097152 | tf_op jit(solution)/shard_map/all_to_all | solution.py:11
  14.8 148.8 %all-gather.12.cloned.1.call-start = ((), (), s32[]{:S(2)}) async-start(), calls=%async_computation.2 | async-start | bytes 17039360 | tf_op jit(solution)/shard_map/all_gather | solution.py:20
  59.4 337.3 %all-gather.14.cloned.1.call-start = ((), (), s32[]{:S(2)}) async-start(), calls=%async_computation.3 | async-start | bytes 17039360 | tf_op jit(solution)/shard_map/all_gather | solution.py:20
  179.1 294.0 %copy-start.2 = (f32[8,4,256]{2,1,0:T(4,128)}, f32[8,4,256]{2,1,0:T(4,128)S(1)}, u32[]{:S(2)}) copy-start(f32[8,4,256]{2,1,0:T(4,128)S(1)} %get-tuple-element.1150) | copy-start | bytes 98308
  473.0 0.7 copy-start.3
Sparse Core Ops, SparseCore 0:
  9.8 29.9 all-gather.9
  59.5 104.1 all-gather.11
  166.5 96.2 all-gather.13
